TPU v7x, 32 devices: a whole 2x2x4 slice. The times are simulated.
32 devices in a mesh: row: 4 (over y, core), col: 8 (over z, x).
Axes of the slice: x: 2, y: 2, z: 4, core: 2. Of those that a mesh axis runs over, the one named last changes fastest.
Arguments:
- acts: bfloat16 [192, 2, 28672], P('col', None, 'row'), may hold values from -6 to 6
- grads: bfloat16 [192, 2, 8192], P('row', None, 'col'), may hold values from -0.3984375 to 0.3984375
- basis_in: bfloat16 [28672, 28672], P('row', 'col'), may hold values from -0.03125 to 0.03125
- basis_out: bfloat16 [8192, 8192], P('col', 'row'), may hold values from -0.0625 to 0.0625
- eigen: bfloat16 [28672, 8192], P('col', 'row'), may hold values from 0.5 to 8
- sketch: bfloat16 [72, 8192], P(None, 'col'), may hold values from -0.0625 to 0.0625
Outputs:
- range_basis: float32 [2, 72, 28672], P(None, None, 'row')
- projected: float32 [2, 72, 8192], P(None, None, 'col')
All inputs are finite; a program needn't handle non-finite values.
Results may differ from a plain program's by a relative error of at most 0.018.
Values may be sent and summed in bfloat16 or wider, within the bound.
A program may use at most 192 MiB of HBM per device.

v0:
```python
import jax
import jax.numpy as jnp
from jax import lax
from jax.sharding import PartitionSpec as P


def on_device(acts, grads, basis_in, basis_out, eigen, sketch):
    full_acts = lax.all_gather(acts, "col", axis=0, tiled=True)
    rows = full_acts
    act_shares = lax.psum_scatter(
        jnp.einsum("tqi,ij->tqj", rows, basis_in, preferred_element_type=jnp.float32),
        "row",
        scatter_dimension=0,
        tiled=True,
    ).astype(jnp.bfloat16)
    full_grads = lax.all_gather(grads, "row", axis=0, tiled=True)
    tokens = full_grads.shape[0]
    queries = full_grads.shape[1]
    flat_grads = full_grads.reshape(tokens * queries, full_grads.shape[2])
    joined = jnp.concatenate([flat_grads, sketch], axis=0)
    joined_sum = lax.psum(
        jnp.dot(joined, basis_out, preferred_element_type=jnp.float32), "col"
    ).astype(jnp.bfloat16)
    grad_rot = joined_sum[: tokens * queries].reshape(tokens, queries, basis_out.shape[1])
    sketch_rot = joined_sum[tokens * queries :]
    rows = grad_rot
    core_sum = jnp.einsum(
        "tqj,tqp->qjp",
        lax.all_gather(act_shares, "row", axis=0, tiled=True),
        rows,
        preferred_element_type=jnp.float32,
    )
    scaled = (core_sum / eigen.astype(jnp.float32)).astype(jnp.bfloat16)
    reduced_part = jnp.einsum("qjp,sp->qsj", scaled, sketch_rot, preferred_element_type=jnp.float32)
    reduced = lax.psum(reduced_part, "row").astype(jnp.bfloat16)
    range_part = jnp.einsum("qsj,ij->qsi", reduced, basis_in, preferred_element_type=jnp.float32)
    range_rows = lax.psum(range_part, "col")
    gram_piece = jnp.einsum("qsi,qri->qsr", range_rows, range_rows, precision=lax.Precision.HIGHEST)
    gram = lax.psum(gram_piece, "row")
    factor = jnp.linalg.cholesky(gram)
    basis_rows = lax.linalg.triangular_solve(factor, range_rows, left_side=True, lower=True)
    mapped_part = jnp.einsum(
        "qsi,ij->qsj", basis_rows.astype(jnp.bfloat16), basis_in, preferred_element_type=jnp.float32
    )
    mapped = lax.psum(mapped_part.astype(jnp.bfloat16), "row")
    core_part = jnp.einsum("qsj,qjp->qsp", mapped, scaled, preferred_element_type=jnp.float32)
    core = lax.psum(core_part.astype(jnp.bfloat16), "col")
    projection_part = jnp.einsum("qsp,op->qso", core, basis_out, preferred_element_type=jnp.float32)
    projected = lax.psum(projection_part.astype(jnp.bfloat16), "row").astype(jnp.float32)
    return (basis_rows, projected)


def solution(mesh):
    in_specs = (
        P("col", None, "row"),
        P("row", None, "col"),
        P("row", "col"),
        P("col", "row"),
        P("col", "row"),
        P(None, "col"),
    )
    out_specs = (P(None, None, "row"), P(None, None, "col"))
    return jax.shard_map(
        on_device, mesh=mesh, in_specs=in_specs, out_specs=out_specs, check_vma=False
    )
```

profile of v0, /device:TPU:0, one launch (start us, length us, event | category | flops | bytes accessed | tf_op | source)
XLA Modules:
  0.0 866.9 jit_solution(3863842434083049462)
XLA Ops:
  7.9 94.1 %all-gather.3.cloned.1.call-done = bf16[192,2,7168]{2,1,0:T(2,128)(2,1)} async-done(((bf16[24,2,7168]{2,1,0:T(2,128)(2,1)}), bf16[192,2,7168]{2,1,0:T(2,128)(2,1)}) %all-gather.3.cloned.1.call-update) | async-done | bytes 5505040 | tf_op jit(solution)/shard_map/all_gather | solution.py:8
  102.0 30.9 %fusion.4 = f32[192,2,3584]{2,0,1:T(8,128)} fusion(bf16[7168,3584]{1,0:T(8,128)(2,1)} %param.8, bf16[192,2,7168]{2,1,0:T(2,128)(2,1)} %all-gather.3.cloned.1.call-done), kind=kOutput, calls=%fused_computation.5 | convolution fusion | flops 19730006016 | bytes 62390272 | tf_op jit(solution)/shard_map/tqi,ij->tqj/dot_general | solution.py:11
  133.0 51.3 %reduce-scatter.2.cloned.1.call-done = f32[48,2,3584]{2,0,1:T(8,128)} async-done(((f32[192,2,3584]{2,0,1:T(8,128)}), f32[48,2,3584]{2,0,1:T(8,128)}) %reduce-scatter.2.cloned.1.call-update) | async-done | bytes 1376272 | tf_op jit(solution)/shard_map/reduce_scatter | solution.py:10
  186.7 8.0 all_gather.9
  195.0 6.2 fusion.18
  201.2 150.4 %all-reduce.14 = bf16[456,2048]{1,0:T(8,128)(2,1)S(1)} all-reduce(f32[456,2048]{1,0:T(8,128)} %fusion.18), channel_id=1, replica_groups=mesh['row'=4,'col'=8] {'col'}, use_global_device_ids=true, to_apply=%region_0.0 | all-reduce | flops 933888 | bytes 5603328 | tf_op jit(solution)/shard_map/psum | solution.py:21
  351.8 2.4 reshape.22
  354.1 16.6 %convert_element_type.32 = f32[3584,2048]{1,0:T(8,128)} convert(bf16[3584,2048]{1,0:T(8,128)(2,1)} %param.10) | non-fusion elementwise | flops 7340032 | bytes 44040192 | tf_op jit(solution)/shard_map/convert_element_type | solution.py:33
  370.8 22.4 %divide_convert_fusion = bf16[2,3584,2048]{2,1,0:T(8,128)(2,1)} fusion(f32[3584,2048]{1,0:T(8,128)} %convert_element_type.32, bf16[192,2,3584]{2,0,1:T(8,128)(2,1)} %all-gather.5.cloned.1.call-done, bf16[192,2,2048]{2,1,0:T(2,128)(2,1)S(1)} %copy-done.2), kind=kOutput, calls=%fused_computation | convolution fusion | flops 5666504704 | bytes 63045632 | tf_op jit(solution)/shard_map/tqj,tqp->qjp/dot_general | solution.py:27
  393.2 14.3 %convolution_bitcast_fusion = f32[2,72,3584]{2,1,0:T(8,128)S(1)} fusion(bf16[2,3584,2048]{2,1,0:T(8,128)(2,1)} %divide_convert_fusion, bf16[456,2048]{1,0:T(8,128)(2,1)} %copy-done.1), kind=kOutput, calls=%fused_computation.8 | convolution fusion | flops 2113929216 | bytes 31719424 | tf_op jit(solution)/shard_map/qjp,sp->qsj/dot_general | solution.py:34
  407.5 39.8 %all-reduce.15 = bf16[2,72,3584]{2,1,0:T(8,128)(2,1)S(1)} all-reduce(f32[2,72,3584]{2,1,0:T(8,128)S(1)} %convolution_bitcast_fusion), channel_id=1, replica_groups=mesh['row'=4,'col'=8] {'row'}, use_global_device_ids=true, to_apply=%region_2.0 | all-reduce | flops 516096 | bytes 3096576 | tf_op jit(solution)/shard_map/psum | solution.py:35
  447.3 26.5 %fusion.2 = f32[2,72,7168]{2,1,0:T(8,128)} fusion(bf16[7168,3584]{1,0:T(8,128)(2,1)} %param.8, bf16[2,72,3584]{2,1,0:T(8,128)(2,1)S(1)} %all-reduce.15), kind=kOutput, calls=%fused_computation.3 | convolution fusion | flops 7398752256 | bytes 56541184 | tf_op jit(solution)/shard_map/qsj,ij->qsi/dot_general | solution.py:36
  474.2 153.0 %all-reduce.7.cloned.1.call-done = f32[2,72,7168]{2,1,0:T(8,128)} async-done(((f32[2,72,7168]{2,1,0:T(8,128)}), f32[2,72,7168]{2,1,0:T(8,128)}) %all-reduce.7.cloned.1.call-update) | async-done | bytes 4128784 | tf_op jit(solution)/shard_map/psum | solution.py:37
  627.2 7.4 fusion.26
  634.6 12.0 %psum.52 = f32[2,72,72]{1,2,0:T(8,128)S(1)} all-reduce(f32[2,72,72]{1,2,0:T(8,128)S(1)} %fusion.26), channel_id=1, replica_groups=mesh['row'=4,'col'=8] {'row'}, use_global_device_ids=true, to_apply=%region_4.0 | all-reduce | flops 10368 | bytes 82944 | tf_op jit(solution)/shard_map/psum | solution.py:39
  646.7 13.2 %custom-call.7 = f32[2,72,72]{2,1,0:T(8,128)S(1)} custom-call(f32[2,72,72]{2,1,0:T(8,128)S(1)} %fusion.24), custom_call_target="Cholesky" | custom-call | tf_op jit(solution)/shard_map/jit(cholesky)/cholesky | solution.py:40
  660.2 11.1 %custom-call.8 = f32[2,1,72,72]{2,3,1,0:T(8,128)S(1)} custom-call(f32[2,1,72,72]{3,2,1,0:T(8,128)S(1)} %select_bitcast_fusion), custom_call_target="InvertDiagBlocksLowerTriangular" | custom-call | tf_op jit(solution)/shard_map/triangular_solve | solution.py:41
  671.3 5.3 fusion.22
  678.6 19.0 %fusion.7 = bf16[2,72,3584]{2,1,0:T(8,128)(2,1)} fusion(bf16[7168,3584]{1,0:T(8,128)(2,1)} %param.8, f32[2,72,7168]{2,1,0:T(8,128)S(1)} %fusion.22), kind=kOutput, calls=%fused_computation.9 | convolution fusion | flops 7400300544 | bytes 56541184 | tf_op jit(solution)/shard_map/qsi,ij->qsj/dot_general | solution.py:42
  698.0 34.3 %all-reduce.9.cloned.1.call-done = bf16[2,72,3584]{2,1,0:T(8,128)(2,1)} async-done(((bf16[2,72,3584]{2,1,0:T(8,128)(2,1)}), bf16[2,72,3584]{2,1,0:T(8,128)(2,1)}) %all-reduce.9.cloned.1.call-update) | async-done | bytes 1032208 | tf_op jit(solution)/shard_map/psum | solution.py:45
  732.3 15.7 %convolution_convert_fusion = bf16[2,72,2048]{2,1,0:T(8,128)(2,1)} fusion(bf16[2,72,3584]{2,1,0:T(8,128)(2,1)} %all-reduce.9.cloned.1.call-done, bf16[2,3584,2048]{2,1,0:T(8,128)(2,1)} %divide_convert_fusion), kind=kOutput, calls=%fused_computation.12 | convolution fusion | flops 2114224128 | bytes 30982144 | tf_op jit(solution)/shard_map/qsj,qjp->qsp/dot_general | solution.py:46
  748.0 74.0 %all-reduce.11.cloned.1.call-done = bf16[2,72,2048]{2,1,0:T(8,128)(2,1)} async-done(((bf16[2,72,2048]{2,1,0:T(8,128)(2,1)}), bf16[2,72,2048]{2,1,0:T(8,128)(2,1)}) %all-reduce.11.cloned.1.call-update) | async-done | bytes 589840 | tf_op jit(solution)/shard_map/psum | solution.py:47
  822.0 4.6 fusion.14
  826.7 31.5 %all-reduce.13.cloned.1.call-done = bf16[2,72,1024]{2,1,0:T(8,128)(2,1)} async-done(((bf16[2,72,1024]{2,1,0:T(8,128)(2,1)}), bf16[2,72,1024]{2,1,0:T(8,128)(2,1)}) %all-reduce.13.cloned.1.call-update) | async-done | bytes 294928 | tf_op jit(solution)/shard_map/psum | solution.py:49
  (36 shorter events, 8.4 us)
Async XLA Ops:
  7.2 94.9 %all-gather.3.cloned.1.call-start = ((), (), s32[]{:S(2)}) async-start(), calls=%async_computation.1 | async-start | bytes 6193152 | tf_op jit(solution)/shard_map/all_gather | solution.py:8
  7.9 176.4 %reduce-scatter.2.cloned.1.call-start = ((), (), s32[]{:S(2)}) async-start(), calls=%async_computation.2 | async-start | bytes 6881280 | tf_op jit(solution)/shard_map/reduce_scatter | solution.py:10
  133.0 53.7 %copy-start.3 = (bf16[48,2,1024]{2,1,0:T(2,128)(2,1)S(1)}, bf16[48,2,1024]{2,1,0:T(2,128)(2,1)}, u32[]{:S(2)}) copy-start(bf16[48,2,1024]{2,1,0:T(2,128)(2,1)} %param.7) | copy-start | bytes 589828
  133.0 62.0 %copy-start.4 = (bf16[72,1024]{1,0:T(8,128)(2,1)S(1)}, bf16[72,1024]{1,0:T(8,128)(2,1)}, u32[]{:S(2)}) copy-start(bf16[72,1024]{1,0:T(8,128)(2,1)} %param.11) | copy-start | bytes 442372
  133.0 237.8 %all-gather.5.cloned.1.call-start = ((), (), s32[]{:S(2)}) async-start(), calls=%async_computation.3 | async-start | bytes 3440640 | tf_op jit(solution)/shard_map/all_gather | solution.py:29
  186.6 440.6 %all-reduce.7.cloned.1.call-start = ((), (), s32[]{:S(2)}) async-start(), calls=%async_computation.4 | async-start | bytes 8257536 | tf_op jit(solution)/shard_map/psum | solution.py:37
  351.6 19.2 %copy-start.1 = (bf16[456,2048]{1,0:T(8,128)(2,1)}, bf16[456,2048]{1,0:T(8,128)(2,1)S(1)}, u32[]{:S(2)}) copy-start(bf16[456,2048]{1,0:T(8,128)(2,1)S(1)} %all-reduce.14) | copy-start | bytes 5603332
  354.1 16.6 %copy-start.2 = (bf16[192,2,2048]{2,1,0:T(2,128)(2,1)S(1)}, bf16[192,2,2048]{2,1,0:T(2,128)(2,1)}, u32[]{:S(2)}) copy-start(bf16[192,2,2048]{2,1,0:T(2,128)(2,1)} %reshape.22) | copy-start | bytes 4718596
  473.9 258.4 %all-reduce.9.cloned.1.call-start = ((), (), s32[]{:S(2)}) async-start(), calls=%async_computation.5 | async-start | bytes 2064384 | tf_op jit(solution)/shard_map/psum | solution.py:45
  676.6 2.0 copy-start
  697.7 124.4 %all-reduce.11.cloned.1.call-start = ((), (), s32[]{:S(2)}) async-start(), calls=%async_computation.6 | async-start | bytes 1179648 | tf_op jit(solution)/shard_map/psum | solution.py:47
  748.0 110.2 %all-reduce.13.cloned.1.call-start = ((), (), s32[]{:S(2)}) async-start(), calls=%async_computation.7 | async-start | bytes 589824 | tf_op jit(solution)/shard_map/psum | solution.py:49
Sparse Core Ops, SparseCore 0:
  10.2 91.8 all-gather.2
  133.1 51.1 reduce-scatter.1
  186.7 26.2 all-gather.4
  474.0 153.1 all-reduce.6
  697.8 34.4 all-reduce.8
  748.1 73.8 all-reduce.10
  826.8 31.3 all-reduce.12
where the time goes:
time: 867 us
  waiting for transfers between devices  439 us (51%)
  blocking collectives  210 us (24%)
  matrix products  153 us (18%)
  other arithmetic  45.3 us (5%)
  between operations  14.3 us (2%)
    psum x1, waiting for transfers between devices, on_device(): range_rows = lax.psum(range_part, 'col')  153 us
    psum x1, blocking collectives, on_device(): lax.psum(jnp.dot(joined, basis_out, preferred_element_type=jnp.float32),...  150 us
    all_gather x1, waiting for transfers between devices, on_device(): full_acts = lax.all_gather(acts, 'col', axis=0, tiled=True)  94.1 us
    psum x1, waiting for transfers between devices, on_device(): core = lax.psum(core_part.astype(jnp.bfloat16), 'col')  74 us
    reduce_scatter x1, waiting for transfers between devices, on_device(): lax.psum_scatter(jnp.einsum('tqi,ij->tqj', rows, basis_in, preferred_elem...  51.3 us
    psum x1, blocking collectives, on_device(): reduced = lax.psum(reduced_part, 'row').astype(jnp.bfloat16)  39.8 us
    psum x1, waiting for transfers between devices, on_device(): mapped = lax.psum(mapped_part.astype(jnp.bfloat16), 'row')  34.3 us
    psum x1, waiting for transfers between devices, on_device(): lax.psum(projection_part.astype(jnp.bfloat16), 'row').astype(jnp.float32)  31.5 us
  transfers between devices with their start and end apart: 7, of which 6 were waited for; matrix products, arithmetic and copies ran while one was open for 3% of the time, Pallas kernels for 0%

commit v1 on v0

v1 whole, which is shorter than its diff:
```python
import functools
import jax
import jax.numpy as jnp
from jax import lax
from jax.experimental import pallas as pl
from jax.experimental.pallas import tpu as pltpu
from jax.sharding import PartitionSpec as P

MESH = pl.DeviceIdType.MESH
VMEM = pl.BlockSpec(memory_space=pltpu.VMEM)
BAND = 16


def greet(axis, n, me):
    barrier = pltpu.get_barrier_semaphore()
    for k in range(1, n):
        pl.semaphore_signal(
            barrier, inc=1, device_id={axis: lax.rem(me + k, n)}, device_id_type=MESH
        )
    pl.semaphore_wait(barrier, n - 1)


def send(src, dst, sems, k, axis, peer):
    copy = pltpu.make_async_remote_copy(
        src_ref=src,
        dst_ref=dst,
        send_sem=sems[0].at[k - 1],
        recv_sem=sems[1].at[k - 1],
        device_id={axis: peer},
        device_id_type=MESH,
    )
    copy.start()
    return copy


def columns(ref, index, width):
    return ref.at[:, pl.ds(pl.multiple_of(index * width, width), width)]


def gather_kernel(axis, n, leading, x_ref, o_ref, send_sem, recv_sem, own_sem):
    me = lax.axis_index(axis)
    place = o_ref.at[me] if leading else columns(o_ref, me, x_ref.shape[1])
    greet(axis, n, me)
    copies = [
        send(x_ref, place, (send_sem, recv_sem), k, axis, lax.rem(me + k, n)) for k in range(1, n)
    ]
    own = pltpu.make_async_copy(x_ref, place, own_sem)
    own.start()
    own.wait()
    for copy in copies:
        copy.wait()


def add_slots(slots, n, out):
    def step(i, carry):
        rows = pl.ds(pl.multiple_of(i * BAND, BAND), BAND)
        total = slots[0, rows, :].astype(jnp.float32)
        for k in range(1, n):
            total = total + slots[k, rows, :].astype(jnp.float32)
        out[rows, :] = total.astype(out.dtype)
        return carry

    lax.fori_loop(0, slots.shape[1] // BAND, step, 0)


def fill_slots(axis, n, me, x_ref, slots, sems, own_sem):
    width = slots.shape[2]
    greet(axis, n, me)
    copies = []
    for k in range(1, n):
        peer = lax.rem(me + k, n)
        copies.append(send(columns(x_ref, peer, width), slots.at[k], sems, k, axis, peer))
    own = pltpu.make_async_copy(columns(x_ref, me, width), slots.at[0], own_sem)
    own.start()
    own.wait()
    for copy in copies:
        copy.wait()


def scatter_kernel(axis, n, x_ref, o_ref, slots, send_sem, recv_sem, own_sem):
    me = lax.axis_index(axis)
    fill_slots(axis, n, me, x_ref, slots, (send_sem, recv_sem), own_sem)
    add_slots(slots, n, o_ref)


def reduce_kernel(
    axis, n, x_ref, o_ref, slots, stage, send_sem, recv_sem, own_sem, send_two, recv_two, own_two
):
    me = lax.axis_index(axis)
    fill_slots(axis, n, me, x_ref, slots, (send_sem, recv_sem), own_sem)
    add_slots(slots, n, stage)
    place = columns(o_ref, me, slots.shape[2])
    copies = [
        send(stage, place, (send_two, recv_two), k, axis, lax.rem(me + k, n)) for k in range(1, n)
    ]
    own = pltpu.make_async_copy(stage, place, own_two)
    own.start()
    own.wait()
    for copy in copies:
        copy.wait()


def semaphores(n):
    return [
        pltpu.SemaphoreType.DMA((n - 1,)),
        pltpu.SemaphoreType.DMA((n - 1,)),
        pltpu.SemaphoreType.DMA,
    ]


def launch(kernel, name, number, shape, dtype, scratch, x):
    return pl.pallas_call(
        kernel,
        name=name,
        out_shape=jax.ShapeDtypeStruct(shape, dtype),
        in_specs=[VMEM],
        out_specs=VMEM,
        scratch_shapes=scratch,
        compiler_params=pltpu.CompilerParams(
            collective_id=number, has_side_effects=True, vmem_limit_bytes=40 * 2**20
        ),
    )(x)


def fits(x, width):
    return x.shape[0] % BAND == 0 and width % 128 == 0


def gather_rows(x, axis, n, number):
    if not fits(x, x.shape[1]):
        return lax.all_gather(x, axis, axis=0, tiled=True)
    kernel = functools.partial(gather_kernel, axis, n, True)
    full = launch(kernel, f"gather{number}", number, (n, *x.shape), x.dtype, semaphores(n), x)
    return full.reshape(n * x.shape[0], x.shape[1])


def gather_columns(x, axis, n, number):
    if not fits(x, x.shape[1]):
        return lax.all_gather(x, axis, axis=1, tiled=True)
    kernel = functools.partial(gather_kernel, axis, n, False)
    shape = (x.shape[0], n * x.shape[1])
    return launch(kernel, f"gather{number}", number, shape, x.dtype, semaphores(n), x)


def scatter_sum(x, axis, n, number):
    width = x.shape[1] // n
    if not fits(x, width):
        return lax.psum_scatter(x.astype(jnp.float32), axis, scatter_dimension=1, tiled=True)
    scratch = [pltpu.VMEM((n, x.shape[0], width), x.dtype), *semaphores(n)]
    kernel = functools.partial(scatter_kernel, axis, n)
    shape = (x.shape[0], width)
    return launch(kernel, f"scatter{number}", number, shape, jnp.float32, scratch, x)


def full_sum(x, axis, n, number):
    width = x.shape[1] // n
    if not fits(x, width):
        return lax.psum(x.astype(jnp.float32), axis).astype(jnp.bfloat16)
    scratch = [
        pltpu.VMEM((n, x.shape[0], width), x.dtype),
        pltpu.VMEM((x.shape[0], width), jnp.bfloat16),
        *semaphores(n),
        *semaphores(n),
    ]
    kernel = functools.partial(reduce_kernel, axis, n)
    return launch(kernel, f"sum{number}", number, x.shape, jnp.bfloat16, scratch, x)


def dot(a, b, contract):
    product = lax.dot_general(a, b, ((contract), ((), ())), preferred_element_type=jnp.float32)
    return product


def on_device(nrow, ncol, acts, grads, basis_in, basis_out, eigen, sketch):
    bf = jnp.bfloat16
    queries = acts.shape[1]
    flat = queries * sketch.shape[0]
    full_acts = gather_rows(acts.reshape(-1, acts.shape[2]), "col", ncol, 0)
    tokens = full_acts.shape[0] // queries
    act_rot = full_sum(dot(full_acts, basis_in, ((1,), (0,))).astype(bf), "row", nrow, 1)
    full_grads = gather_rows(grads.reshape(-1, grads.shape[2]), "row", nrow, 2)
    joined = jnp.concatenate([full_grads, sketch], axis=0)
    joined = jnp.pad(joined, ((0, -joined.shape[0] % BAND), (0, 0)))
    joined_sum = full_sum(dot(joined, basis_out, ((1,), (0,))).astype(bf), "col", ncol, 3)
    grad_rot = joined_sum[: tokens * queries].reshape(tokens, queries, -1)
    sketch_rot = joined_sum[tokens * queries : tokens * queries + sketch.shape[0]]
    core_sum = jnp.einsum(
        "tqj,tqp->qjp",
        act_rot.reshape(tokens, queries, -1),
        grad_rot,
        preferred_element_type=jnp.float32,
    )
    scaled = (core_sum / eigen.astype(jnp.float32)).astype(bf)
    reduced_part = jnp.einsum("qjp,sp->qsj", scaled, sketch_rot, preferred_element_type=jnp.float32)
    reduced = full_sum(reduced_part.astype(bf).reshape(flat, -1), "row", nrow, 4)
    range_part = dot(reduced, basis_in, ((1,), (1,))).astype(bf)
    range_rows = scatter_sum(range_part, "col", ncol, 5).reshape(queries, sketch.shape[0], -1)
    gram_piece = jnp.einsum("qsi,qri->qsr", range_rows, range_rows, precision=lax.Precision.HIGHEST)
    gram = lax.psum(gram_piece, ("row", "col"))
    factor = jnp.linalg.cholesky(gram)
    basis_piece = lax.linalg.triangular_solve(factor, range_rows, left_side=True, lower=True)
    basis_rows = gather_columns(basis_piece.astype(bf).reshape(flat, -1), "col", ncol, 6)
    mapped_part = dot(basis_rows, basis_in, ((1,), (0,))).astype(bf)
    mapped = full_sum(mapped_part, "row", nrow, 7).reshape(queries, sketch.shape[0], -1)
    core_part = jnp.einsum("qsj,qjp->qsp", mapped, scaled, preferred_element_type=jnp.float32)
    core = full_sum(core_part.astype(bf).reshape(flat, -1), "col", ncol, 8)
    projection_part = dot(core, basis_out, ((1,), (1,))).astype(bf)
    projected = full_sum(projection_part, "row", nrow, 9)
    shape = (queries, sketch.shape[0], -1)
    return (
        basis_rows.astype(jnp.float32).reshape(shape),
        projected.astype(jnp.float32).reshape(shape),
    )


def solution(mesh):
    in_specs = (
        P("col", None, "row"),
        P("row", None, "col"),
        P("row", "col"),
        P("col", "row"),
        P("col", "row"),
        P(None, "col"),
    )
    out_specs = (P(None, None, "row"), P(None, None, "col"))
    body = functools.partial(on_device, mesh.shape["row"], mesh.shape["col"])
    return jax.shard_map(body, mesh=mesh, in_specs=in_specs, out_specs=out_specs, check_vma=False)
```

time: 867 us -> 698 us (0.81)
  Pallas kernels: 0 us -> 464 us
  waiting for transfers between devices: 439 us -> 0 us
  blocking collectives: 210 us -> 53.6 us
  matrix products: 153 us -> 123 us
  between operations: 14.3 us -> 0.87 us
    pallas_call x0 -> x10, Pallas kernels: none -> 464 us  [launch(): pl.pallas_call(kernel, name=name, out_shape=jax.ShapeDtypeStruct(shape, d...]
    psum x4 -> x0, waiting for transfers between devices: 293 us -> none  [the longest x1 153 us: on_device(): range_rows = lax.psum(range_part, 'col')]
    psum x3 -> x1, blocking collectives: 202 us -> 53.6 us  [on_device(): gram = lax.psum(gram_piece, ('row', 'col'))]
    all_gather x2 -> x0, waiting for transfers between devices: 94.1 us -> none  [the longest x1 94.1 us: on_device(): full_acts = lax.all_gather(acts, 'col', axis=0, tiled=True)]
    reduce_scatter x1 -> x0, waiting for transfers between devices: 51.3 us -> none  [on_device(): lax.psum_scatter(jnp.einsum('tqi,ij->tqj', rows, basis_in, preferred_elem...]
    dot_general x6, matrix products: 110 us -> 94.8 us  [the longest x5 72 us: dot(): lax.dot_general(a, b, (contract, ((), ())), preferred_element_type=jnp.fl...]
    convert_element_type x3 -> x1, other arithmetic: 20.7 us -> 16.6 us  [on_device(): scaled = (core_sum / eigen.astype(jnp.float32)).astype(bf)]
  transfers between devices with their start and end apart: 7 -> 0, of which waited for: 6 -> 0; matrix products, arithmetic and copies ran while one was open for 3% -> 0% of each run, Pallas kernels for 0% -> 0%
where the time goes in v1:
time: 698 us; the launch traced here: 694 us
  Pallas kernels  464 us (66%)
  matrix products  123 us (18%)
  blocking collectives  53.6 us (8%)
  other arithmetic  44.5 us (6%)
  local copies, waits for them, and re-layouts  8.48 us (1%)
    pallas_call x10, Pallas kernels, launch(): pl.pallas_call(kernel, name=name, out_shape=jax.ShapeDtypeStruct(shape, d...  464 us
    dot_general x5, matrix products, dot(): lax.dot_general(a, b, (contract, ((), ())), preferred_element_type=jnp.fl...  72 us
    psum x1, blocking collectives, on_device(): gram = lax.psum(gram_piece, ('row', 'col'))  53.6 us
    dot_general x1, matrix products, on_device(): jnp.einsum('tqj,tqp->qjp', act_rot.reshape(tokens, queries, -1), grad_rot...  22.8 us
    convert_element_type x1, other arithmetic, on_device(): scaled = (core_sum / eigen.astype(jnp.float32)).astype(bf)  16.6 us
    dot_general x1, matrix products, on_device(): jnp.einsum('qjp,sp->qsj', scaled, sketch_rot, preferred_element_type=jnp....  14.3 us

profile of v1, /device:TPU:0, one launch (start us, length us, event | category | flops | bytes accessed | tf_op | source)
XLA Modules:
  0.0 694.4 jit_solution(4478717053639674216)
XLA Ops:
  1.6 12.1 %gather2.1 = bf16[4,96,1024]{2,1,0:T(8,128)(2,1)S(1)} custom-call(bf16[96,1024]{1,0:T(8,128)(2,1)S(1)} %reshape.60.x_ref), custom_call_target="tpu_custom_call" | custom-call | tf_op jit(solution)/shard_map/gather2/pallas_call | solution.py:112
  13.7 4.4 convolution_convert_fusion.4.x_ref
  18.1 83.9 %sum3.1 = bf16[464,2048]{1,0:T(8,128)(2,1)S(1)} custom-call(bf16[464,2048]{1,0:T(8,128)(2,1)S(1)} %convolution_convert_fusion.4.x_ref), custom_call_target="tpu_custom_call" | custom-call | tf_op jit(solution)/shard_map/sum3/pallas_call | solution.py:112
  103.4 2.3 reshape.65
  105.7 16.6 %convert_element_type.39 = f32[3584,2048]{1,0:T(8,128)} convert(bf16[3584,2048]{1,0:T(8,128)(2,1)} %param.10) | non-fusion elementwise | flops 7340032 | bytes 44040192 | tf_op jit(solution)/shard_map/convert_element_type | solution.py:193
  122.5 104.1 %gather0.1 = bf16[8,48,7168]{2,1,0:T(8,128)(2,1)S(1)} custom-call(bf16[48,7168]{1,0:T(8,128)(2,1)S(1)} %reshape.62.x_ref), custom_call_target="tpu_custom_call" | custom-call | tf_op jit(solution)/shard_map/gather0/pallas_call | solution.py:112
  226.6 25.5 %convolution_convert_fusion.1.x_ref = bf16[384,3584]{1,0:T(8,128)(2,1)S(1)} fusion(bf16[384,7168]{1,0:T(8,128)(2,1)S(1)} %bitcast.45, bf16[7168,3584]{1,0:T(8,128)(2,1)} %param.8), kind=kOutput, calls=%fused_computation.2 | convolution fusion | flops 19731382272 | bytes 59637760 | tf_op jit(solution)/shard_map/dot_general | solution.py:170
  252.2 61.3 %sum1.1 = bf16[384,3584]{1,0:T(8,128)(2,1)S(1)} custom-call(bf16[384,3584]{1,0:T(8,128)(2,1)S(1)} %convolution_convert_fusion.1.x_ref), custom_call_target="tpu_custom_call" | custom-call | tf_op jit(solution)/shard_map/sum1/pallas_call | solution.py:112
  313.5 2.5 reshape.64
  316.0 22.8 %divide_convert_fusion = bf16[2,3584,2048]{2,1,0:T(8,128)(2,1)} fusion(f32[3584,2048]{1,0:T(8,128)} %convert_element_type.39, bf16[192,2,3584]{2,1,0:T(2,128)(2,1)} %reshape.64, bf16[192,2,2048]{2,1,0:T(2,128)(2,1)} %reshape.65), kind=kOutput, calls=%fused_computation | convolution fusion | flops 5666504704 | bytes 63045632 | tf_op jit(solution)/shard_map/tqj,tqp->qjp/dot_general | solution.py:187
  338.7 14.3 %convolution_convert_fusion.3 = bf16[72,2,3584]{2,0,1:T(8,128)(2,1)S(1)} fusion(bf16[2,3584,2048]{2,1,0:T(8,128)(2,1)} %divide_convert_fusion, bf16[464,2048]{1,0:T(8,128)(2,1)} %copy-done), kind=kOutput, calls=%fused_computation.4 | convolution fusion | flops 2114445312 | bytes 30687232 | tf_op jit(solution)/shard_map/qjp,sp->qsj/dot_general | solution.py:194
  353.1 26.0 %sum4.1 = bf16[144,3584]{1,0:T(8,128)(2,1)S(1)} custom-call(bf16[144,3584]{1,0:T(8,128)(2,1)S(1)} %bitcast.42), custom_call_target="tpu_custom_call" | custom-call | tf_op jit(solution)/shard_map/sum4/pallas_call | solution.py:112
  380.0 22.5 %convolution_convert_fusion.x_ref = bf16[144,7168]{1,0:T(8,128)(2,1)S(1)} fusion(bf16[144,3584]{1,0:T(8,128)(2,1)} %copy-done.1, bf16[7168,3584]{1,0:T(8,128)(2,1)} %param.8), kind=kOutput, calls=%fused_computation.1 | convolution fusion | flops 7399784448 | bytes 54476800 | tf_op jit(solution)/shard_map/dot_general | solution.py:170
  402.5 67.2 %scatter5.1 = f32[144,896]{1,0:T(8,128)S(1)} custom-call(bf16[144,7168]{1,0:T(8,128)(2,1)S(1)} %convolution_convert_fusion.x_ref), custom_call_target="tpu_custom_call" | custom-call | tf_op jit(solution)/shard_map/scatter5/pallas_call | solution.py:112
  470.3 53.6 %psum.7 = f32[2,72,72]{1,2,0:T(8,128)S(1)} all-reduce(f32[2,72,72]{1,2,0:T(8,128)S(1)} %fusion.18), channel_id=1, replica_groups=mesh['row'=4,'col'=8] {'row','col'}, use_global_device_ids=true, to_apply=%region_0.1 | all-reduce | flops 10368 | bytes 82944 | tf_op jit(solution)/shard_map/psum | solution.py:199
  524.0 13.2 %custom-call.7 = f32[2,72,72]{2,1,0:T(8,128)S(1)} custom-call(f32[2,72,72]{2,1,0:T(8,128)S(1)} %fusion.14), custom_call_target="Cholesky" | custom-call | tf_op jit(solution)/shard_map/jit(cholesky)/cholesky | solution.py:200
  537.5 11.1 %custom-call.8 = f32[2,1,72,72]{2,3,1,0:T(8,128)S(1)} custom-call(f32[2,1,72,72]{3,2,1,0:T(8,128)S(1)} %select_bitcast_fusion), custom_call_target="InvertDiagBlocksLowerTriangular" | custom-call | tf_op jit(solution)/shard_map/triangular_solve | solution.py:201
  549.3 35.1 %gather6.1 = bf16[144,7168]{1,0:T(8,128)(2,1)S(1)} custom-call(bf16[144,896]{1,0:T(8,128)(2,1)S(1)} %bitcast.48), custom_call_target="tpu_custom_call" | custom-call | tf_op jit(solution)/shard_map/gather6/pallas_call | solution.py:112
  584.4 18.1 %convolution_convert_fusion.2.x_ref = bf16[144,3584]{1,0:T(8,128)(2,1)S(1)} fusion(bf16[144,7168]{1,0:T(8,128)(2,1)S(1)} %gather6.1, bf16[7168,3584]{1,0:T(8,128)(2,1)} %param.8), kind=kOutput, calls=%fused_computation.3 | convolution fusion | flops 7399268352 | bytes 54476800 | tf_op jit(solution)/shard_map/dot_general | solution.py:170
  602.5 25.8 %sum7.1 = bf16[144,3584]{1,0:T(8,128)(2,1)S(1)} custom-call(bf16[144,3584]{1,0:T(8,128)(2,1)S(1)} %convolution_convert_fusion.2.x_ref), custom_call_target="tpu_custom_call" | custom-call | tf_op jit(solution)/shard_map/sum7/pallas_call | solution.py:112
  628.3 12.3 %convolution_convert_fusion.5 = bf16[2,72,2048]{2,1,0:T(8,128)(2,1)S(1)} fusion(bf16[2,72,3584]{2,1,0:T(8,128)(2,1)S(1)} %bitcast.41, bf16[2,3584,2048]{2,1,0:T(8,128)(2,1)} %divide_convert_fusion), kind=kOutput, calls=%fused_computation.7 | convolution fusion | flops 2114224128 | bytes 30982144 | tf_op jit(solution)/shard_map/qsj,qjp->qsp/dot_general | solution.py:205
  640.6 39.4 %sum8.1 = bf16[144,2048]{1,0:T(8,128)(2,1)S(1)} custom-call(bf16[144,2048]{1,0:T(8,128)(2,1)S(1)} %bitcast.46), custom_call_target="tpu_custom_call" | custom-call | tf_op jit(solution)/shard_map/sum8/pallas_call | solution.py:112
  681.6 9.5 %sum9.1 = bf16[144,1024]{1,0:T(8,128)(2,1)S(1)} custom-call(bf16[144,1024]{1,0:T(8,128)(2,1)S(1)} %convolution_convert_fusion.6.x_ref), custom_call_target="tpu_custom_call" | custom-call | tf_op jit(solution)/shard_map/sum9/pallas_call | solution.py:112
  692.0 2.4 convert.2
  (22 shorter events, 7.7 us)
Async XLA Ops:
  102.0 1.3 copy-start
  105.7 16.6 %copy-start.3 = (bf16[24,2,7168]{2,1,0:T(2,128)(2,1)S(1)}, bf16[24,2,7168]{2,1,0:T(2,128)(2,1)}, u32[]{:S(2)}) copy-start(bf16[24,2,7168]{2,1,0:T(2,128)(2,1)} %param.6) | copy-start | bytes 2064388
  379.1 1.0 copy-start.1
  628.3 51.7 %copy-start.2 = (bf16[1024,2048]{1,0:T(8,128)(2,1)S(1)}, bf16[1024,2048]{1,0:T(8,128)(2,1)}, u32[]{:S(2)}) copy-start(bf16[1024,2048]{1,0:T(8,128)(2,1)} %param.9) | copy-start | bytes 12582916
